TPU v7x, 32 devices: a whole 2x2x4 slice. The times are simulated.
32 devices in a mesh: slab: 8 (over z, core), split: 4 (over y, x).
Axes of the slice: x: 2, y: 2, z: 4, core: 2. Of those that a mesh axis runs over, the one named last changes fastest.
Arguments:
- displacement: float32 [3, 64, 128, 256], P(None, 'slab', 'split'), may hold values from -0.3 to 0.3
- velocity: float32 [3, 64, 128, 256], P(None, 'slab', 'split'), may hold values from -0.6 to 0.6
- acceleration: float32 [3, 64, 128, 256], P(None, 'slab', 'split'), may hold values from -1.8 to 1.8
- bond_masks: int32 [4, 64, 128, 256], P(None, 'slab', 'split'), may hold values from 0 to 255, as said below
- proj_pos: float32 [32, 3, 128], replicated, may hold values from -0.5 to 257, as said below
- proj_vel: float32 [32, 3, 128], replicated, may hold values from -1.8 to 1.8
- proj_acc: float32 [32, 3, 128], replicated, may hold values from -1.8 to 1.8
- contact_pairs: int32 [3, 2, 512], P(None, None, ('slab', 'split')), may hold values from -1 to 31, as said below
Outputs:
- final_displacement: float32 [3, 64, 128, 256], P(None, 'slab', 'split')
- final_velocity: float32 [3, 64, 128, 256], P(None, 'slab', 'split')
- final_proj_pos: float32 [32, 3, 128], replicated
- final_proj_vel: float32 [32, 3, 128], replicated
Inputs may be any that keep to these rules, and one draw needn't show every extreme that they name: `bond_masks`: bit b of word w (the value divided by 2 to the b, modulo 2) is 1 where the bond from the cell to the offset numbered 8 w + b is intact. `contact_pairs`: slots d * 16 to (d + 1) * 16 - 1 belong to device d. Row 0 names one of that device's 8 surface blocks; row 1 names a projectile block, or -1 for an empty slot. Live slots come first on every device and no pair repeats on a device within a substep. In every substep each projectile block is paired on exactly one device, one of the four devices of the 2 x 2 group of device blocks under it, and on another device than in the substep before; in every substep some device has all 16 slots live. `proj_pos`: the device blocks fall into 2 x 2 groups (slab indices 2a and 2a + 1, split indices 2b and 2b + 1). Every projectile block lies above one such group, between 0.5 and 2 cells over the top layer, and every group lies under exactly 4 projectile blocks.
All inputs are finite; a program needn't handle non-finite values.
Results may differ from a plain program's by a relative error of at most 0.0003.
Values sent between devices are 32-bit elements; how exact they have to be, the bound alone decides.
A program may use at most 128 MiB of HBM per device.

v0:
```python
import math
import jax
import jax.numpy as jnp
from jax import lax
from jax.sharding import PartitionSpec as P

SUB = 3
SL = 4
PTS = 128
SB_DEV = 8
time_step = 0.25
bond_stiffness = 0.5
contact_stiffness = 0.05
contact_width = 8.0
inverse_mass = 0.5


def with_halo(cells, sides, width):
    for axis, dim in sides:
        count = lax.axis_size(axis)
        ends = count - 1
        head = lax.slice_in_dim(cells, 0, width, axis=dim)
        tail = lax.slice_in_dim(cells, cells.shape[dim] - width, cells.shape[dim], axis=dim)
        cells = jnp.concatenate(
            [
                lax.ppermute(tail, axis, [(i, (i + 1) % count) for i in range(ends)]),
                cells,
                lax.ppermute(head, axis, [((i + 1) % count, i) for i in range(ends)]),
            ],
            axis=dim,
        )
    return cells


def bond_offsets():
    listed = []
    for shift_x in (-2, -1, 0, 1, 2):
        for shift_y in (-2, -1, 0, 1, 2):
            for shift_z in (-2, -1, 0, 1, 2):
                squared = shift_x * shift_x + shift_y * shift_y + shift_z * shift_z
                if 0 < squared <= 4:
                    listed.append((shift_x, shift_y, shift_z))
    return listed


def bond_term(neighbour, displace, intact, valid_bond, offset):
    shift_x, shift_y, shift_z = offset
    length = math.sqrt(shift_x * shift_x + shift_y * shift_y + shift_z * shift_z)
    along_x = shift_x + (neighbour[0] - displace[0])
    along_y = shift_y + (neighbour[1] - displace[1])
    along_z = shift_z + (neighbour[2] - displace[2])
    squared = along_x * along_x + along_y * along_y + along_z * along_z
    stretch = (squared - length * length) / (length * (jnp.sqrt(squared) + length))
    return bond_stiffness / length * stretch * intact * valid_bond


def add_bond(bond_total, coefficient, offset):
    direction = jnp.array(offset, bond_total.dtype)
    return bond_total + direction[:, None, None, None] * coefficient[None]


def shift_depth(values_in, shift_size):
    if shift_size == 0:
        return values_in
    filler = jnp.zeros(values_in.shape[:-1] + (abs(shift_size),), values_in.dtype)
    if shift_size > 0:
        return jnp.concatenate([values_in[..., shift_size:], filler], axis=-1)
    return jnp.concatenate([filler, values_in[..., :shift_size]], axis=-1)


def bond_forces(padded, displace, mask_words, inside_x, inside_y):
    cells_x, cells_y, cells_z = (displace.shape[1], displace.shape[2], displace.shape[3])
    depth_index = jnp.arange(cells_z)
    bond_total = jnp.zeros_like(displace)
    for number, offset in enumerate(bond_offsets()):
        shift_x, shift_y, shift_z = offset
        window = padded[
            :, 2 + shift_x : 2 + shift_x + cells_x, 2 + shift_y : 2 + shift_y + cells_y, :
        ]
        neighbour = shift_depth(window, shift_z)
        moved_depth = depth_index + shift_z
        inside_z = ((moved_depth >= 0) & (moved_depth < cells_z)).astype(jnp.float32)
        valid_bond = (
            inside_x[2 + shift_x : 2 + shift_x + cells_x][:, None, None]
            * inside_y[2 + shift_y : 2 + shift_y + cells_y][None, :, None]
            * inside_z[None, None, :]
        )
        intact = (mask_words[number // 8] // 2 ** (number % 8) % 2).astype(jnp.float32)
        bond_total = add_bond(
            bond_total, bond_term(neighbour, displace, intact, valid_bond, offset), offset
        )
    return bond_total


def contact_tile(points, particles):
    separation = points[:, :, None] - particles[:, None, :]
    squared = jnp.sum(separation * separation, axis=0)
    weight = contact_stiffness * jnp.exp(-squared / contact_width)
    pulled = weight[None] * separation
    return (jnp.sum(pulled, axis=2), -jnp.sum(pulled, axis=1))


def slot_tiles(slot_points, chosen, positions):
    picked = positions[jnp.maximum(chosen, 0)]
    on_points, on_particles = jax.vmap(contact_tile)(slot_points, picked)
    live = (chosen >= 0).astype(jnp.float32)[:, None, None]
    return (on_points * live, on_particles * live)


def per_device(
    displacement, velocity, acceleration, bond_masks, proj_pos, proj_vel, proj_acc, contact_pairs
):
    cells_x, cells_y, cells_z = (
        displacement.shape[1],
        displacement.shape[2],
        displacement.shape[3],
    )
    slab_count = lax.axis_size("slab")
    split_count = lax.axis_size("split")
    corner_x = lax.axis_index("slab") * cells_x
    corner_y = lax.axis_index("split") * cells_y
    span_x = jnp.arange(-2, cells_x + 2) + corner_x
    span_y = jnp.arange(-2, cells_y + 2) + corner_y
    inside_x = ((span_x >= 0) & (span_x < slab_count * cells_x)).astype(jnp.float32)
    inside_y = ((span_y >= 0) & (span_y < split_count * cells_y)).astype(jnp.float32)
    place_x = (corner_x + jnp.arange(cells_x)).astype(jnp.float32)
    place_y = (corner_y + jnp.arange(cells_y)).astype(jnp.float32)
    place_z = (cells_z - SL + jnp.arange(SL)).astype(jnp.float32)
    lattice = jnp.stack(
        [
            jnp.broadcast_to(place_x[:, None, None], (cells_x, cells_y, SL)),
            jnp.broadcast_to(place_y[None, :, None], (cells_x, cells_y, SL)),
            jnp.broadcast_to(place_z[None, None, :], (cells_x, cells_y, SL)),
        ]
    )
    blocks_total = proj_pos.shape[0]
    particle_slots = jnp.arange(blocks_total)
    block_slots = jnp.arange(SB_DEV)
    for substep in range(SUB):
        half_velocity = velocity + 0.5 * time_step * acceleration
        displacement = displacement + time_step * half_velocity
        proj_half = proj_vel + 0.5 * time_step * proj_acc
        proj_pos = proj_pos + time_step * proj_half
        padded = with_halo(displacement, (("slab", 1), ("split", 2)), 2)
        forces = bond_forces(padded, displacement, bond_masks, inside_x, inside_y)
        top_layers = displacement[:, :, :, cells_z - SL :]
        places = (top_layers + lattice).reshape(3, SB_DEV, PTS)
        slot_pairs = contact_pairs[substep]
        targets = slot_pairs[0]
        chosen = slot_pairs[1]
        slot_points = jnp.moveaxis(jnp.take(places, targets, axis=1), 1, 0)
        on_points, on_particles = slot_tiles(slot_points, chosen, proj_pos)
        target_hits = (targets[:, None] == block_slots[None, :]).astype(jnp.float32)
        surface = jnp.einsum("ks,kcp->csp", target_hits, on_points, precision=lax.Precision.HIGHEST)
        forces = forces + jnp.pad(
            surface.reshape(3, cells_x, cells_y, SL), ((0, 0), (0, 0), (0, 0), (cells_z - SL, 0))
        )
        particle_hits = (chosen[:, None] == particle_slots[None, :]).astype(jnp.float32)
        particle_local = jnp.einsum(
            "kb,kcp->bcp", particle_hits, on_particles, precision=lax.Precision.HIGHEST
        )
        acceleration = forces
        velocity = half_velocity + 0.5 * time_step * acceleration
        particle_force = lax.psum(particle_local, ("slab", "split"))
        proj_acc = inverse_mass * particle_force
        proj_vel = proj_half + 0.5 * time_step * proj_acc
    return (displacement, velocity, proj_pos, proj_vel)


def solution(mesh):
    placed = (
        P(None, "slab", "split", None),
        P(None, "slab", "split", None),
        P(None, "slab", "split", None),
        P(None, "slab", "split", None),
        P(),
        P(),
        P(),
        P(None, None, ("slab", "split")),
    )
    return jax.shard_map(
        per_device,
        mesh=mesh,
        in_specs=placed,
        out_specs=(P(None, "slab", "split", None), P(None, "slab", "split", None), P(), P()),
        check_vma=False,
    )
```

profile of v0, /device:TPU:4, one launch (start us, length us, event | category | flops | bytes accessed | tf_op | source)
XLA Modules:
  0.0 280.0 jit_solution(2510947669306366044)
XLA Ops:
  0.6 1.8 multiply_add_fusion.3
  3.2 1.3 collective-permute-start.1
  4.5 3.0 %collective-permute-start = (f32[3,2,32,256]{3,2,1,0:T(8,128)S(1)}, f32[3,2,32,256]{3,2,1,0:T(8,128)S(1)}, u32[]{:S(2)}, u32[]{:S(2)}) collective-permute-start(f32[3,2,32,256]{3,2,1,0:T(8,128)S(1)} %get-tuple-element.217), channel_id=1, source_target_pairs={{0,4},{4,8},{8,12},{12,16},{16,20},{20,24},{24,28},{1,5},{5,9},{9,... | collective-permute-start | bytes 589832 | tf_op jit(solution)/shard_map/ppermute | solution.py:26
  10.4 1.4 fusion.1172
  14.5 1.0 fusion.6
  15.8 2.0 fusion
  18.2 1.4 copy.483
  20.0 41.7 %psum.21 = f32[32,3,128]{2,0,1:T(8,128)S(1)} all-reduce(f32[32,3,128]{2,0,1:T(8,128)S(1)} %fusion.1136), channel_id=1, replica_groups=mesh['slab'=8,'split'=4] {'slab','split'}, use_global_device_ids=true, to_apply=%region_3.5 | all-reduce | flops 12288 | bytes 98304 | tf_op jit(solution)/shard_map/psum | solution.py:164
  64.2 1.2 gather_fusion.1
  65.7 3.3 %collective-permute-start.3 = (f32[3,12,2,256]{3,2,1,0:T(2,128)S(1)}, f32[3,12,2,256]{3,2,1,0:T(2,128)S(1)}, u32[]{:S(2)}, u32[]{:S(2)}) collective-permute-start(f32[3,12,2,256]{3,2,1,0:T(2,128)S(1)} %get-tuple-element.190), channel_id=1, source_target_pairs={{1,0},{2,1},{3,2},{5,4},{6,5},{7,6},{9,8},{10,9},{11,10},{13,12},{... | collective-permute-start | bytes 221192 | tf_op jit(solution)/shard_map/ppermute | solution.py:28
  69.0 3.0 %collective-permute-start.2 = (f32[3,12,2,256]{3,2,1,0:T(2,128)S(1)}, f32[3,12,2,256]{3,2,1,0:T(2,128)S(1)}, u32[]{:S(2)}, u32[]{:S(2)}) collective-permute-start(f32[3,12,2,256]{3,2,1,0:T(2,128)S(1)} %get-tuple-element.191), channel_id=1, source_target_pairs={{0,1},{1,2},{2,3},{4,5},{5,6},{6,7},{8,9},{9,10},{10,11},{12,13},{... | collective-permute-start | bytes 221192 | tf_op jit(solution)/shard_map/ppermute | solution.py:26
  72.0 2.5 fusion.16
  74.5 1.2 select_maximum_fusion.2
  76.4 2.9 %fusion.1166 = (f32[3,8,32,255]{3,2,1,0:T(8,128)S(1)}, f32[3,8,32,255]{3,2,1,0:T(8,128)S(1)}, f32[3,8,32,255]{3,2,1,0:T(8,128)S(1)}, f32[3,8,32,255]{3,2,1,0:T(8...) fusion(f32[3,12,34,256]{3,2,1,0:T(8,128)S(1)} %get-tuple-elemen, ...), kind=kLoop, calls=%fused_computation.1893 | loop fusion | bytes 18800640 | tf_op jit(solution)/shard_map/slice | solution.py:68
  79.3 1.9 fusion.102
  86.3 1.1 fusion.111
  87.4 1.0 fusion.171
  90.4 1.1 fusion.135
  98.9 3.3 %multiply_add_fusion.2 = (f32[3,8,32,256]{3,2,1,0:T(8,128)S(1)}, f32[3,8,32,256]{3,2,1,0:T(8,128)}) fusion(f32[3,8,32,256]{3,2,1,0:T(8,128)S(1)} %multiply_add_fusion.3, f32[3,8,32,4]{3,2,1,0:T(8,128)S(1)} %copy-done.17, f32[8,32,256]{2,1,0:T(8,128)S(1)} %get-tuple-element.69, f32[3]{0:T(128)S(1)} %copy-done.74, f32[8,32,256]{2,1,0:T(8,128)S(1)} %get-tuple-element.119, ...), kind=kLoop, calls=%fused_computation.134 | loop fusion | flops 13565952 | bytes 12333416 | tf_op jit(solution)/shard_map/add | solution.py:141
  104.7 1.0 fusion.7
  106.0 2.7 fusion.2
  109.0 1.4 copy.491
  110.4 1.3 collective-permute-start.5
  111.7 3.0 %collective-permute-start.4 = (f32[3,2,32,256]{3,2,1,0:T(8,128)}, f32[3,2,32,256]{3,2,1,0:T(8,128)S(1)}, u32[]{:S(2)}, u32[]{:S(2)}) collective-permute-start(f32[3,2,32,256]{3,2,1,0:T(8,128)} %get-tuple-element.210), channel_id=1, source_target_pairs={{0,4},{4,8},{8,12},{12,16},{16,20},{20,24},{24,28},{1,5},{5,9},{9,... | collective-permute-start | bytes 589832 | tf_op jit(solution)/shard_map/ppermute | solution.py:26
  114.7 1.0 fusion.1133
  115.8 41.2 %psum.22 = f32[32,3,128]{2,0,1:T(8,128)S(1)} all-reduce(f32[32,3,128]{2,0,1:T(8,128)S(1)} %fusion.1133), channel_id=1, replica_groups=mesh['slab'=8,'split'=4] {'slab','split'}, use_global_device_ids=true, to_apply=%region_7.9 | all-reduce | flops 12288 | bytes 98304 | tf_op jit(solution)/shard_map/psum | solution.py:164
  157.1 1.3 gather_fusion.2
  158.8 2.9 %collective-permute-start.6 = (f32[3,12,2,256]{3,2,1,0:T(2,128)S(1)}, f32[3,12,2,256]{3,2,1,0:T(2,128)S(1)}, u32[]{:S(2)}, u32[]{:S(2)}) collective-permute-start(f32[3,12,2,256]{3,2,1,0:T(2,128)S(1)} %get-tuple-element.186), channel_id=1, source_target_pairs={{0,1},{1,2},{2,3},{4,5},{5,6},{6,7},{8,9},{9,10},{10,11},{12,13},{... | collective-permute-start | bytes 221192 | tf_op jit(solution)/shard_map/ppermute | solution.py:26
  161.8 4.2 %collective-permute-start.7 = (f32[3,12,2,256]{3,2,1,0:T(2,128)S(1)}, f32[3,12,2,256]{3,2,1,0:T(2,128)S(1)}, u32[]{:S(2)}, u32[]{:S(2)}) collective-permute-start(f32[3,12,2,256]{3,2,1,0:T(2,128)S(1)} %get-tuple-element.187), channel_id=1, source_target_pairs={{1,0},{2,1},{3,2},{5,4},{6,5},{7,6},{9,8},{10,9},{11,10},{13,12},{... | collective-permute-start | bytes 221192 | tf_op jit(solution)/shard_map/ppermute | solution.py:28
  177.8 1.2 fusion.172
  179.9 1.0 fusion.112
  185.7 3.4 %multiply_add_fusion.1 = (f32[3,8,32,256]{3,2,1,0:T(8,128)S(1)}, f32[3,8,32,256]{3,2,1,0:T(8,128)}) fusion(f32[3,8,32,256]{3,2,1,0:T(8,128)S(1)} %get-tuple-element.31, f32[3,8,32,256]{3,2,1,0:T(8,128)S(1)} %copy-done.4, f32[3,8,32,4]{3,2,1,0:T(8,128)S(1)} %copy-done.18, f32[8,32,256]{2,1,0:T(8,128)S(1)} %get-tuple-element.67, f32[3]{0:T(128)S(1)} %copy-done.75, ...), kind=kLoop, calls=%fused_computation.133 | loop fusion | flops 13172736 | bytes 11546984 | tf_op jit(solution)/shard_map/add | solution.py:141
  190.8 1.1 fusion.1168
  192.0 1.3 copy.493
  193.3 1.0 copy.494
  195.8 1.8 fusion.8
  197.7 2.6 fusion.4
  200.7 1.4 copy.499
  202.1 1.3 collective-permute-start.9
  203.4 3.0 %collective-permute-start.8 = (f32[3,2,32,256]{3,2,1,0:T(8,128)}, f32[3,2,32,256]{3,2,1,0:T(8,128)S(1)}, u32[]{:S(2)}, u32[]{:S(2)}) collective-permute-start(f32[3,2,32,256]{3,2,1,0:T(8,128)} %get-tuple-element.203), channel_id=1, source_target_pairs={{0,4},{4,8},{8,12},{12,16},{16,20},{20,24},{24,28},{1,5},{5,9},{9,... | collective-permute-start | bytes 589832 | tf_op jit(solution)/shard_map/ppermute | solution.py:26
  206.4 1.7 fusion.1130
  208.1 39.7 %psum.23 = f32[32,3,128]{2,0,1:T(8,128)} all-reduce(f32[32,3,128]{2,0,1:T(8,128)} %fusion.1130), channel_id=1, replica_groups=mesh['slab'=8,'split'=4] {'slab','split'}, use_global_device_ids=true, to_apply=%region_11.13 | all-reduce | flops 12288 | bytes 98304 | tf_op jit(solution)/shard_map/psum | solution.py:164
  247.8 1.5 multiply_add_fusion.5
  249.3 3.7 %collective-permute-start.10 = (f32[3,12,2,256]{3,2,1,0:T(2,128)S(1)}, f32[3,12,2,256]{3,2,1,0:T(2,128)S(1)}, u32[]{:S(2)}, u32[]{:S(2)}) collective-permute-start(f32[3,12,2,256]{3,2,1,0:T(2,128)S(1)} %get-tuple-element.182), channel_id=1, source_target_pairs={{0,1},{1,2},{2,3},{4,5},{5,6},{6,7},{8,9},{9,10},{10,11},{12,13},{... | collective-permute-start | bytes 221192 | tf_op jit(solution)/shard_map/ppermute | solution.py:26
  253.0 3.3 %collective-permute-start.11 = (f32[3,12,2,256]{3,2,1,0:T(2,128)S(1)}, f32[3,12,2,256]{3,2,1,0:T(2,128)S(1)}, u32[]{:S(2)}, u32[]{:S(2)}) collective-permute-start(f32[3,12,2,256]{3,2,1,0:T(2,128)S(1)} %get-tuple-element.183), channel_id=1, source_target_pairs={{1,0},{2,1},{3,2},{5,4},{6,5},{7,6},{9,8},{10,9},{11,10},{13,12},{... | collective-permute-start | bytes 221192 | tf_op jit(solution)/shard_map/ppermute | solution.py:28
  268.3 1.3 fusion.173
  272.4 1.1 fusion.128
  276.2 3.4 %multiply_add_fusion = f32[3,8,32,256]{3,2,1,0:T(8,128)} fusion(f32[3,8,32,256]{3,2,1,0:T(8,128)S(1)} %copy-done.3, f32[3,8,32,4]{3,2,1,0:T(8,128)S(1)} %copy-done.16, f32[8,32,256]{2,1,0:T(8,128)S(1)} %get-tuple-element.89, f32[8,32,256]{2,1,0:T(8,128)S(1)} %get-tuple-element.121, f32[8,32,256]{2,1,0:T(8,128)S(1)} %get-tuple-element.65, ...), kind=kLoop, calls=%fused_computation.132 | loop fusion | flops 12582912 | bytes 9974120 | tf_op jit(solution)/shard_map/add | solution.py:163
  (477 shorter events, 64.9 us)
Async XLA Ops:
  0.6 6.9 %copy-start.73 = (s32[3,2,16]{2,1,0:T(2,128)S(1)}, s32[3,2,16]{2,1,0:T(2,128)}, u32[]{:S(2)}) copy-start(s32[3,2,16]{2,1,0:T(2,128)} %param.113) | copy-start | bytes 1156
  3.2 62.4 %collective-permute-start.1 = (f32[3,2,32,256]{3,2,1,0:T(8,128)}, f32[3,2,32,256]{3,2,1,0:T(8,128)S(1)}, u32[]{:S(2)}, u32[]{:S(2)}) collective-permute-start(f32[3,2,32,256]{3,2,1,0:T(8,128)} %get-tuple-element.218), channel_id=1, source_target_pairs={{4,0},{8,4},{12,8},{16,12},{20,16},{24,20},{28,24},{5,1},{9,5},{13... | collective-permute-start | bytes 589832 | tf_op jit(solution)/shard_map/ppermute | solution.py:28
  4.5 61.1 %collective-permute-start = (f32[3,2,32,256]{3,2,1,0:T(8,128)S(1)}, f32[3,2,32,256]{3,2,1,0:T(8,128)S(1)}, u32[]{:S(2)}, u32[]{:S(2)}) collective-permute-start(f32[3,2,32,256]{3,2,1,0:T(8,128)S(1)} %get-tuple-element.217), channel_id=1, source_target_pairs={{0,4},{4,8},{8,12},{12,16},{16,20},{20,24},{24,28},{1,5},{5,9},{9,... | collective-permute-start | bytes 589832 | tf_op jit(solution)/shard_map/ppermute | solution.py:26
  11.8 49.9 %copy-start.20 = (f32[32,3,128]{2,0,1:T(8,128)}, f32[32,3,128]{2,0,1:T(8,128)S(1)}, u32[]{:S(2)}) copy-start(f32[32,3,128]{2,0,1:T(8,128)S(1)} %multiply_add_fusion.8) | copy-start | bytes 147460
  15.6 2.3 copy-start.174
  15.6 2.3 copy-start.175
  15.8 3.9 %copy-start.72 = (f32[36]{0:T(128)S(1)}, f32[36]{0:T(128)}, u32[]{:S(2)}) copy-start(f32[36]{0:T(128)} %and_convert_fusion.4) | copy-start | bytes 436
  15.8 4.0 %copy-start.173 = (s32[16]{0:T(128)S(1)}, s32[16]{0:T(128)}, u32[]{:S(2)}) copy-start(s32[16]{0:T(128)} %get-tuple-element.220) | copy-start | bytes 196
  15.8 46.6 %copy-start.166 = (s32[16]{0:T(128)S(1)}, s32[16]{0:T(128)}, u32[]{:S(2)}) copy-start(s32[16]{0:T(128)} %get-tuple-element.222) | copy-start | bytes 196
  15.8 46.6 %copy-start.168 = (s32[16]{0:T(128)S(1)}, s32[16]{0:T(128)}, u32[]{:S(2)}) copy-start(s32[16]{0:T(128)} %get-tuple-element.230) | copy-start | bytes 196
  15.8 47.2 %copy-start.165 = (s32[16]{0:T(128)S(1)}, s32[16]{0:T(128)}, u32[]{:S(2)}) copy-start(s32[16]{0:T(128)} %get-tuple-element.226) | copy-start | bytes 196
  15.8 47.8 %copy-start.167 = (s32[16]{0:T(128)S(1)}, s32[16]{0:T(128)}, u32[]{:S(2)}) copy-start(s32[16]{0:T(128)} %get-tuple-element.24) | copy-start | bytes 196
  65.5 13.8 %copy-start.59 = (f32[8,32]{1,0:T(8,128)}, f32[8,32]{1,0:T(8,128)S(1)}, u32[]{:S(2)}) copy-start(f32[8,32]{1,0:T(8,128)S(1)} %get-tuple-element.247) | copy-start | bytes 3076
  65.5 18.3 %copy-start.47 = (f32[8,32]{1,0:T(8,128)}, f32[8,32]{1,0:T(8,128)S(1)}, u32[]{:S(2)}) copy-start(f32[8,32]{1,0:T(8,128)S(1)} %get-tuple-element.242) | copy-start | bytes 3076
  65.5 21.9 %copy-start.41 = (f32[8,32]{1,0:T(8,128)}, f32[8,32]{1,0:T(8,128)S(1)}, u32[]{:S(2)}) copy-start(f32[8,32]{1,0:T(8,128)S(1)} %get-tuple-element.240) | copy-start | bytes 3076
  65.5 22.9 %copy-start.56 = (f32[8,32]{1,0:T(8,128)}, f32[8,32]{1,0:T(8,128)S(1)}, u32[]{:S(2)}) copy-start(f32[8,32]{1,0:T(8,128)S(1)} %get-tuple-element.245) | copy-start | bytes 3076
  65.5 23.9 %copy-start.35 = (f32[8,32]{1,0:T(8,128)}, f32[8,32]{1,0:T(8,128)S(1)}, u32[]{:S(2)}) copy-start(f32[8,32]{1,0:T(8,128)S(1)} %get-tuple-element.243) | copy-start | bytes 3076
  65.5 24.9 %copy-start.53 = (f32[8,32]{1,0:T(8,128)}, f32[8,32]{1,0:T(8,128)S(1)}, u32[]{:S(2)}) copy-start(f32[8,32]{1,0:T(8,128)S(1)} %get-tuple-element.237) | copy-start | bytes 3076
  65.5 26.0 %copy-start.32 = (f32[8,32]{1,0:T(8,128)}, f32[8,32]{1,0:T(8,128)S(1)}, u32[]{:S(2)}) copy-start(f32[8,32]{1,0:T(8,128)S(1)} %get-tuple-element.238) | copy-start | bytes 3076
  65.5 27.0 %copy-start.26 = (f32[8,32]{1,0:T(8,128)}, f32[8,32]{1,0:T(8,128)S(1)}, u32[]{:S(2)}) copy-start(f32[8,32]{1,0:T(8,128)S(1)} %get-tuple-element.236) | copy-start | bytes 3076
  65.5 28.4 %copy-start.38 = (f32[8,32]{1,0:T(8,128)}, f32[8,32]{1,0:T(8,128)S(1)}, u32[]{:S(2)}) copy-start(f32[8,32]{1,0:T(8,128)S(1)} %get-tuple-element.239) | copy-start | bytes 3076
  65.5 29.4 %copy-start.29 = (f32[8,32]{1,0:T(8,128)}, f32[8,32]{1,0:T(8,128)S(1)}, u32[]{:S(2)}) copy-start(f32[8,32]{1,0:T(8,128)S(1)} %get-tuple-element.244) | copy-start | bytes 3076
  65.5 30.5 %copy-start.62 = (f32[8,32]{1,0:T(8,128)}, f32[8,32]{1,0:T(8,128)S(1)}, u32[]{:S(2)}) copy-start(f32[8,32]{1,0:T(8,128)S(1)} %get-tuple-element.246) | copy-start | bytes 3076
  65.6 31.3 %copy-start.44 = (f32[8,32]{1,0:T(8,128)}, f32[8,32]{1,0:T(8,128)S(1)}, u32[]{:S(2)}) copy-start(f32[8,32]{1,0:T(8,128)S(1)} %get-tuple-element.235) | copy-start | bytes 3076
  65.7 10.0 %collective-permute-start.3 = (f32[3,12,2,256]{3,2,1,0:T(2,128)S(1)}, f32[3,12,2,256]{3,2,1,0:T(2,128)S(1)}, u32[]{:S(2)}, u32[]{:S(2)}) collective-permute-start(f32[3,12,2,256]{3,2,1,0:T(2,128)S(1)} %get-tuple-element.190), channel_id=1, source_target_pairs={{1,0},{2,1},{3,2},{5,4},{6,5},{7,6},{9,8},{10,9},{11,10},{13,12},{... | collective-permute-start | bytes 221192 | tf_op jit(solution)/shard_map/ppermute | solution.py:28
  69.0 7.1 %collective-permute-start.2 = (f32[3,12,2,256]{3,2,1,0:T(2,128)S(1)}, f32[3,12,2,256]{3,2,1,0:T(2,128)S(1)}, u32[]{:S(2)}, u32[]{:S(2)}) collective-permute-start(f32[3,12,2,256]{3,2,1,0:T(2,128)S(1)} %get-tuple-element.191), channel_id=1, source_target_pairs={{0,1},{1,2},{2,3},{4,5},{5,6},{6,7},{8,9},{9,10},{10,11},{12,13},{... | collective-permute-start | bytes 221192 | tf_op jit(solution)/shard_map/ppermute | solution.py:26
  76.4 2.9 %copy-start.1 = (s32[4,8,32,256]{3,2,1,0:T(8,128)S(1)}, s32[4,8,32,256]{3,2,1,0:T(8,128)}, u32[]{:S(2)}) copy-start(s32[4,8,32,256]{3,2,1,0:T(8,128)} %param.109) | copy-start | bytes 3145732
  79.3 1.9 copy-start.11
  102.2 2.5 copy-start.164
  102.2 2.6 copy-start.24
  105.8 2.9 %copy-start.171 = (f32[16]{0:T(128)S(1)}, f32[16]{0:T(128)}, u32[]{:S(2)}) copy-start(f32[16]{0:T(128)} %get-tuple-element.231) | copy-start | bytes 196
  105.8 2.9 %copy-start.172 = (s32[16]{0:T(128)S(1)}, s32[16]{0:T(128)}, u32[]{:S(2)}) copy-start(s32[16]{0:T(128)} %get-tuple-element.223) | copy-start | bytes 196
  106.0 51.0 %copy-start.21 = (f32[32,3,128]{2,0,1:T(8,128)S(1)}, f32[32,3,128]{2,0,1:T(8,128)}, u32[]{:S(2)}) copy-start(f32[32,3,128]{2,0,1:T(8,128)} %copy-done.20) | copy-start | bytes 147460
  106.0 51.0 %copy-start.22 = (f32[32,3,128]{2,0,1:T(8,128)S(1)}, f32[32,3,128]{2,0,1:T(8,128)}, u32[]{:S(2)}) copy-start(f32[32,3,128]{2,0,1:T(8,128)} %get-tuple-element.30) | copy-start | bytes 147460
  110.4 48.3 %collective-permute-start.5 = (f32[3,2,32,256]{3,2,1,0:T(8,128)}, f32[3,2,32,256]{3,2,1,0:T(8,128)S(1)}, u32[]{:S(2)}, u32[]{:S(2)}) collective-permute-start(f32[3,2,32,256]{3,2,1,0:T(8,128)} %get-tuple-element.211), channel_id=1, source_target_pairs={{4,0},{8,4},{12,8},{16,12},{20,16},{24,20},{28,24},{5,1},{9,5},{13... | collective-permute-start | bytes 589832 | tf_op jit(solution)/shard_map/ppermute | solution.py:28
  111.7 47.1 %collective-permute-start.4 = (f32[3,2,32,256]{3,2,1,0:T(8,128)}, f32[3,2,32,256]{3,2,1,0:T(8,128)S(1)}, u32[]{:S(2)}, u32[]{:S(2)}) collective-permute-start(f32[3,2,32,256]{3,2,1,0:T(8,128)} %get-tuple-element.210), channel_id=1, source_target_pairs={{0,4},{4,8},{8,12},{12,16},{16,20},{20,24},{24,28},{1,5},{5,9},{9,... | collective-permute-start | bytes 589832 | tf_op jit(solution)/shard_map/ppermute | solution.py:26
  157.0 9.7 %copy-start.23 = (f32[32,3,128]{2,0,1:T(8,128)}, f32[32,3,128]{2,0,1:T(8,128)S(1)}, u32[]{:S(2)}) copy-start(f32[32,3,128]{2,0,1:T(8,128)S(1)} %psum.22) | copy-start | bytes 147460
  157.1 1.7 copy-start.52
  158.8 14.0 %collective-permute-start.6 = (f32[3,12,2,256]{3,2,1,0:T(2,128)S(1)}, f32[3,12,2,256]{3,2,1,0:T(2,128)S(1)}, u32[]{:S(2)}, u32[]{:S(2)}) collective-permute-start(f32[3,12,2,256]{3,2,1,0:T(2,128)S(1)} %get-tuple-element.186), channel_id=1, source_target_pairs={{0,1},{1,2},{2,3},{4,5},{5,6},{6,7},{8,9},{9,10},{10,11},{12,13},{... | collective-permute-start | bytes 221192 | tf_op jit(solution)/shard_map/ppermute | solution.py:26
  161.8 11.0 %collective-permute-start.7 = (f32[3,12,2,256]{3,2,1,0:T(2,128)S(1)}, f32[3,12,2,256]{3,2,1,0:T(2,128)S(1)}, u32[]{:S(2)}, u32[]{:S(2)}) collective-permute-start(f32[3,12,2,256]{3,2,1,0:T(2,128)S(1)} %get-tuple-element.187), channel_id=1, source_target_pairs={{1,0},{2,1},{3,2},{5,4},{6,5},{7,6},{9,8},{10,9},{11,10},{13,12},{... | collective-permute-start | bytes 221192 | tf_op jit(solution)/shard_map/ppermute | solution.py:28
  189.0 85.4 %copy-start = (f32[3,8,32,256]{3,2,1,0:T(8,128)}, f32[3,8,32,256]{3,2,1,0:T(8,128)S(1)}, u32[]{:S(2)}) copy-start(f32[3,8,32,256]{3,2,1,0:T(8,128)S(1)} %get-tuple-element.25) | copy-start | bytes 2359300
  195.7 2.0 copy-start.25
  197.5 2.8 %copy-start.169 = (f32[16]{0:T(128)S(1)}, f32[16]{0:T(128)}, u32[]{:S(2)}) copy-start(f32[16]{0:T(128)} %get-tuple-element.228) | copy-start | bytes 196
  197.5 2.8 %copy-start.170 = (s32[16]{0:T(128)S(1)}, s32[16]{0:T(128)}, u32[]{:S(2)}) copy-start(s32[16]{0:T(128)} %get-tuple-element.227) | copy-start | bytes 196
  202.1 47.1 %collective-permute-start.9 = (f32[3,2,32,256]{3,2,1,0:T(8,128)}, f32[3,2,32,256]{3,2,1,0:T(8,128)S(1)}, u32[]{:S(2)}, u32[]{:S(2)}) collective-permute-start(f32[3,2,32,256]{3,2,1,0:T(8,128)} %get-tuple-element.204), channel_id=1, source_target_pairs={{4,0},{8,4},{12,8},{16,12},{20,16},{24,20},{28,24},{5,1},{9,5},{13... | collective-permute-start | bytes 589832 | tf_op jit(solution)/shard_map/ppermute | solution.py:28
  203.4 45.9 %collective-permute-start.8 = (f32[3,2,32,256]{3,2,1,0:T(8,128)}, f32[3,2,32,256]{3,2,1,0:T(8,128)S(1)}, u32[]{:S(2)}, u32[]{:S(2)}) collective-permute-start(f32[3,2,32,256]{3,2,1,0:T(8,128)} %get-tuple-element.203), channel_id=1, source_target_pairs={{0,4},{4,8},{8,12},{12,16},{16,20},{20,24},{24,28},{1,5},{5,9},{9,... | collective-permute-start | bytes 589832 | tf_op jit(solution)/shard_map/ppermute | solution.py:26
  249.3 13.9 %collective-permute-start.10 = (f32[3,12,2,256]{3,2,1,0:T(2,128)S(1)}, f32[3,12,2,256]{3,2,1,0:T(2,128)S(1)}, u32[]{:S(2)}, u32[]{:S(2)}) collective-permute-start(f32[3,12,2,256]{3,2,1,0:T(2,128)S(1)} %get-tuple-element.182), channel_id=1, source_target_pairs={{0,1},{1,2},{2,3},{4,5},{5,6},{6,7},{8,9},{9,10},{10,11},{12,13},{... | collective-permute-start | bytes 221192 | tf_op jit(solution)/shard_map/ppermute | solution.py:26
  253.0 10.2 %collective-permute-start.11 = (f32[3,12,2,256]{3,2,1,0:T(2,128)S(1)}, f32[3,12,2,256]{3,2,1,0:T(2,128)S(1)}, u32[]{:S(2)}, u32[]{:S(2)}) collective-permute-start(f32[3,12,2,256]{3,2,1,0:T(2,128)S(1)} %get-tuple-element.183), channel_id=1, source_target_pairs={{1,0},{2,1},{3,2},{5,4},{6,5},{7,6},{9,8},{10,9},{11,10},{13,12},{... | collective-permute-start | bytes 221192 | tf_op jit(solution)/shard_map/ppermute | solution.py:28
  (140 other events, 178.4 us)
where the time goes:
time: 285 us; the launch traced here: 280 us
  blocking collectives  123 us (43%)
  other arithmetic  86.3 us (30%)
  starting transfers between devices  33.4 us (12%)
  local copies, waits for them, and re-layouts  29.6 us (10%)
  between operations  4.09 us (1%)
  matrix products  3.59 us (1%)
    psum x3, blocking collectives, per_device(): particle_force = lax.psum(particle_local, ('slab', 'split'))  123 us
    mul x49, other arithmetic, add_bond(): return bond_total + direction[:, None, None, None] * coefficient[None]  47.1 us
    ppermute x6, starting transfers between devices, with_halo(): lax.ppermute(tail, axis, [(i, (i + 1) % count) for i in range(ends)])  18.8 us
    ppermute x6, starting transfers between devices, with_halo(): lax.ppermute(head, axis, [((i + 1) % count, i) for i in range(ends)])  14.6 us
    add x3, other arithmetic, per_device(): displacement = displacement + time_step * half_velocity  8.5 us
    slice x7, local copies, waits for them, and re-layouts, shift_depth(): return jnp.concatenate([filler, values_in[..., :shift_size]], axis=-1)  8.44 us
    reduce_sum x3, other arithmetic, contact_tile(): return (jnp.sum(pulled, axis=2), -jnp.sum(pulled, axis=1))  7.3 us
    concatenate x10, other arithmetic, with_halo(): jnp.concatenate([lax.ppermute(tail, axis, [(i, (i + 1) % count) for i in...  6.48 us
  transfers between devices with their start and end apart: 12, of which 1 were waited for; matrix products, arithmetic and copies ran while one was open for 14% of the time, Pallas kernels for 0%

commit v1 on v0

--- a/solution.py
+++ b/solution.py
@@ -161,7 +161,7 @@
         )
         acceleration = forces
         velocity = half_velocity + 0.5 * time_step * acceleration
-        particle_force = lax.psum(particle_local, ("slab", "split"))
+        particle_force = jnp.sum(lax.all_gather(particle_local, ("slab", "split")), axis=0)
         proj_acc = inverse_mass * particle_force
         proj_vel = proj_half + 0.5 * time_step * proj_acc
     return (displacement, velocity, proj_pos, proj_vel)

time: 285 us -> 270 us (0.947)
  the two profiles are of different devices: /device:TPU:4 before, /device:TPU:0 now
where the time goes in v1:
time: 270 us; the launch traced here: 265 us
  other arithmetic  123 us (46%)
  waiting for transfers between devices  56.9 us (21%)
  starting transfers between devices  33.9 us (13%)
  local copies, waits for them, and re-layouts  32.1 us (12%)
  between operations  16.4 us (6%)
  matrix products  3.32 us (1%)
    mul x49, other arithmetic, add_bond(): return bond_total + direction[:, None, None, None] * coefficient[None]  71.6 us
    all_gather x3, waiting for transfers between devices, per_device(): lax.all_gather(particle_local, ('slab', 'split'))  56.8 us
    ppermute x6, starting transfers between devices, with_halo(): lax.ppermute(tail, axis, [(i, (i + 1) % count) for i in range(ends)])  25.6 us
    slice x7, local copies, waits for them, and re-layouts, shift_depth(): return jnp.concatenate([filler, values_in[..., :shift_size]], axis=-1)  11.1 us
    add x3, other arithmetic, per_device(): displacement = displacement + time_step * half_velocity  11.1 us
    ppermute x6, starting transfers between devices, with_halo(): lax.ppermute(head, axis, [((i + 1) % count, i) for i in range(ends)])  8.11 us
    reduce_sum x3, other arithmetic, contact_tile(): return (jnp.sum(pulled, axis=2), -jnp.sum(pulled, axis=1))  7.34 us
    add x1, other arithmetic, per_device(): velocity = half_velocity + 0.5 * time_step * acceleration  6.91 us
  transfers between devices with their start and end apart: 15, of which 2 were waited for; matrix products, arithmetic and copies ran while one was open for 46% of the time, Pallas kernels for 0%

profile of v1, /device:TPU:0, one launch (start us, length us, event | category | flops | bytes accessed | tf_op | source)
XLA Modules:
  0.0 265.5 jit_solution(9253597896889141393)
XLA Ops:
  7.3 1.8 multiply_add_fusion.3
  11.1 3.0 %collective-permute-start = (f32[3,2,32,256]{3,2,1,0:T(8,128)S(1)}, f32[3,2,32,256]{3,2,1,0:T(8,128)S(1)}, u32[]{:S(2)}, u32[]{:S(2)}) collective-permute-start(f32[3,2,32,256]{3,2,1,0:T(8,128)S(1)} %get-tuple-element.217), channel_id=1, source_target_pairs={{0,4},{4,8},{8,12},{12,16},{16,20},{20,24},{24,28},{1,5},{5,9},{9,... | collective-permute-start | bytes 589832 | tf_op jit(solution)/shard_map/ppermute | solution.py:26
  19.3 2.0 fusion
  31.4 6.0 %collective-permute-start.2 = (f32[3,12,2,256]{3,2,1,0:T(2,128)S(1)}, f32[3,12,2,256]{3,2,1,0:T(2,128)S(1)}, u32[]{:S(2)}, u32[]{:S(2)}) collective-permute-start(f32[3,12,2,256]{3,2,1,0:T(2,128)S(1)} %get-tuple-element.191), channel_id=1, source_target_pairs={{0,1},{1,2},{2,3},{4,5},{5,6},{6,7},{8,9},{9,10},{10,11},{12,13},{... | collective-permute-start | bytes 221192 | tf_op jit(solution)/shard_map/ppermute | solution.py:26
  37.4 2.5 fusion.16
  41.4 2.6 fusion.1166
  62.5 3.3 %multiply_add_fusion.2 = (f32[3,8,32,256]{3,2,1,0:T(8,128)S(1)}, f32[3,8,32,256]{3,2,1,0:T(8,128)}) fusion(f32[3,8,32,256]{3,2,1,0:T(8,128)S(1)} %multiply_add_fusion.3, f32[3,8,32,4]{3,2,1,0:T(8,128)S(1)} %copy-done.45, f32[8,32,256]{2,1,0:T(8,128)S(1)} %get-tuple-element.69, f32[3]{0:T(128)S(1)} %copy-done.113, f32[8,32,256]{2,1,0:T(8,128)S(1)} %get-tuple-element.119, ...), kind=kLoop, calls=%fused_computation.134 | loop fusion | flops 13565952 | bytes 12333416 | tf_op jit(solution)/shard_map/add | solution.py:141
  70.8 3.7 %collective-permute-start.4 = (f32[3,2,32,256]{3,2,1,0:T(8,128)S(1)}, f32[3,2,32,256]{3,2,1,0:T(8,128)S(1)}, u32[]{:S(2)}, u32[]{:S(2)}) collective-permute-start(f32[3,2,32,256]{3,2,1,0:T(8,128)S(1)} %get-tuple-element.210), channel_id=1, source_target_pairs={{0,4},{4,8},{8,12},{12,16},{16,20},{20,24},{24,28},{1,5},{5,9},{9,... | collective-permute-start | bytes 589832 | tf_op jit(solution)/shard_map/ppermute | solution.py:26
  76.8 4.3 %collective-permute-start.6 = (f32[3,12,2,256]{3,2,1,0:T(2,128)S(1)}, f32[3,12,2,256]{3,2,1,0:T(2,128)S(1)}, u32[]{:S(2)}, u32[]{:S(2)}) collective-permute-start(f32[3,12,2,256]{3,2,1,0:T(2,128)S(1)} %get-tuple-element.186), channel_id=1, source_target_pairs={{0,1},{1,2},{2,3},{4,5},{5,6},{6,7},{8,9},{9,10},{10,11},{12,13},{... | collective-permute-start | bytes 221192 | tf_op jit(solution)/shard_map/ppermute | solution.py:26
  83.4 1.7 fusion.181
  85.1 1.8 fusion.148
  87.5 1.7 fusion.118
  89.2 1.7 fusion.184
  96.2 1.7 fusion.178
  99.5 1.7 fusion.160
  101.2 1.7 fusion.139
  102.9 2.1 fusion.190
  105.1 1.7 fusion.136
  106.8 1.7 fusion.108
  108.5 1.8 fusion.172
  110.3 1.8 fusion.112
  112.1 1.8 fusion.163
  118.1 2.7 %fusion.2 = (f32[16,3,128]{2,1,0:T(4,128)}, f32[16,3,128]{2,1,0:T(4,128)S(1)}) fusion(f32[16,128,128]{2,1,0:T(8,128)S(1)} %exponential_multiply_fusion.1, f32[16,3,128]{2,1,0:T(4,128)S(1)} %gather_fusion.1, f32[16,3,128]{2,1,0:T(4,128)S(1)} %broadcast_select_fusion.1), kind=kLoop, calls=%fused_computation.14 | loop fusion | flops 3133440 | bytes 1146880 | tf_op jit(solution)/shard_map/vmap()/reduce_sum | solution.py:100
  122.4 6.0 %multiply_add_fusion.1 = (f32[3,8,32,256]{3,2,1,0:T(8,128)S(1)}, f32[3,8,32,256]{3,2,1,0:T(8,128)}) fusion(f32[3,8,32,256]{3,2,1,0:T(8,128)S(1)} %get-tuple-element.31, f32[3,8,32,256]{3,2,1,0:T(8,128)} %get-tuple-element.32, f32[3,8,32,4]{3,2,1,0:T(8,128)} %copy.503, f32[8,32,256]{2,1,0:T(8,128)} %get-tuple-element.67, f32[3]{0:T(128)} %constant.1031.clone, ...), kind=kLoop, calls=%fused_computation.133 | loop fusion | flops 13172736 | bytes 11546984 | tf_op jit(solution)/shard_map/add | solution.py:141
  133.2 4.4 %collective-permute-start.8 = (f32[3,2,32,256]{3,2,1,0:T(8,128)S(1)}, f32[3,2,32,256]{3,2,1,0:T(8,128)S(1)}, u32[]{:S(2)}, u32[]{:S(2)}) collective-permute-start(f32[3,2,32,256]{3,2,1,0:T(8,128)S(1)} %get-tuple-element.203), channel_id=1, source_target_pairs={{0,4},{4,8},{8,12},{12,16},{16,20},{20,24},{24,28},{1,5},{5,9},{9,... | collective-permute-start | bytes 589832 | tf_op jit(solution)/shard_map/ppermute | solution.py:26
  139.1 4.3 %collective-permute-start.10 = (f32[3,12,2,256]{3,2,1,0:T(2,128)S(1)}, f32[3,12,2,256]{3,2,1,0:T(2,128)S(1)}, u32[]{:S(2)}, u32[]{:S(2)}) collective-permute-start(f32[3,12,2,256]{3,2,1,0:T(2,128)S(1)} %get-tuple-element.182), channel_id=1, source_target_pairs={{0,1},{1,2},{2,3},{4,5},{5,6},{6,7},{8,9},{9,10},{10,11},{12,13},{... | collective-permute-start | bytes 221192 | tf_op jit(solution)/shard_map/ppermute | solution.py:26
  145.6 1.7 fusion.182
  147.3 1.8 fusion.149
  151.0 1.7 fusion.119
  152.7 1.7 fusion.185
  156.3 2.1 fusion.1162
  158.5 1.7 fusion.179
  160.1 2.4 fusion.1163
  162.5 1.7 fusion.161
  164.2 1.7 fusion.140
  165.9 25.1 %all-gather.9.cloned.1.call-done = f32[1024,3,128]{2,0,1:T(8,128)} async-done(((f32[32,3,128]{2,0,1:T(8,128)}), f32[1024,3,128]{2,0,1:T(8,128)}) %all-gather.9.cloned.1.call-update) | async-done | bytes 1572880 | tf_op jit(solution)/shard_map/all_gather | solution.py:164
  191.1 2.1 reduce_sum.115
  196.8 2.0 fusion.8
  199.0 2.7 %fusion.4 = (f32[16,3,128]{2,1,0:T(4,128)S(1)}, f32[16,3,128]{2,1,0:T(4,128)}) fusion(f32[16,128,128]{2,1,0:T(8,128)S(1)} %exponential_multiply_fusion, f32[16,3,128]{2,1,0:T(4,128)S(1)} %gather_fusion.2, f32[16,3,128]{2,1,0:T(4,128)S(1)} %copy-done.57), kind=kLoop, calls=%fused_computation.16 | loop fusion | flops 3133440 | bytes 1146880 | tf_op jit(solution)/shard_map/vmap()/reduce_sum | solution.py:100
  202.7 2.9 %fusion.131 = (f32[8,32,256]{2,1,0:T(8,128)}, f32[8,32,256]{2,1,0:T(8,128)}) fusion(f32[3,12,34,256]{3,2,1,0:T(8,128)S(1)} %get-tuple-element.181, f32[8,32]{1,0:T(8,128)S(1)} %copy-done.63, f32[256]{0:T(256)S(1)} %copy-done.54, f32[3,8,32,256]{3,2,1,0:T(8,128)S(1)} %get-tuple-element.25, pred[1,8,32,256]{3,2,1,0:T(8,128)(4,1)} %copy-done.4, ...), kind=kLoop, calls=%fused_computation.696 | loop fusion | flops 4325376 | bytes 3276800 | tf_op jit(solution)/shard_map/mul | solution.py:59
  205.8 1.7 fusion.191
  207.5 1.8 fusion.137
  209.4 1.8 fusion.128
  211.2 1.7 fusion.173
  213.0 1.8 fusion.113
  215.0 1.8 fusion.164
  217.9 6.9 %multiply_add_fusion = f32[3,8,32,256]{3,2,1,0:T(8,128)} fusion(f32[3,8,32,256]{3,2,1,0:T(8,128)} %get-tuple-element.26, f32[3,8,32,4]{3,2,1,0:T(8,128)S(1)} %copy.511, f32[8,32,256]{2,1,0:T(8,128)} %get-tuple-element.89, f32[8,32,256]{2,1,0:T(8,128)} %get-tuple-element.121, f32[8,32,256]{2,1,0:T(8,128)} %get-tuple-element.65, ...), kind=kLoop, calls=%fused_computation.132 | loop fusion | flops 12582912 | bytes 9974120 | tf_op jit(solution)/shard_map/add | solution.py:163
  224.9 31.7 %all-gather.11.cloned.1.call-done = f32[1024,3,128]{2,0,1:T(8,128)} async-done(((f32[32,3,128]{2,0,1:T(8,128)}), f32[1024,3,128]{2,0,1:T(8,128)}) %all-gather.11.cloned.1.call-update) | async-done | bytes 1572880 | tf_op jit(solution)/shard_map/all_gather | solution.py:164
  (478 shorter events, 79.5 us)
Async XLA Ops:
  7.2 7.0 %copy-start.112 = (s32[3,2,16]{2,1,0:T(2,128)S(1)}, s32[3,2,16]{2,1,0:T(2,128)}, u32[]{:S(2)}) copy-start(s32[3,2,16]{2,1,0:T(2,128)} %param.113) | copy-start | bytes 1156
  7.2 8.2 %copy-start.103 = (f32[32,3,128]{2,0,1:T(8,128)S(1)}, f32[32,3,128]{2,0,1:T(8,128)}, u32[]{:S(2)}) copy-start(f32[32,3,128]{2,0,1:T(8,128)} %param.110) | copy-start | bytes 147460
  7.2 8.2 %copy-start.86 = (f32[32,3,128]{2,0,1:T(8,128)S(1)}, f32[32,3,128]{2,0,1:T(8,128)}, u32[]{:S(2)}) copy-start(f32[32,3,128]{2,0,1:T(8,128)} %param.111) | copy-start | bytes 147460
  7.2 8.2 %copy-start.88 = (f32[32,3,128]{2,0,1:T(8,128)S(1)}, f32[32,3,128]{2,0,1:T(8,128)}, u32[]{:S(2)}) copy-start(f32[32,3,128]{2,0,1:T(8,128)} %param.112) | copy-start | bytes 147460
  7.2 106.6 %all-gather.7.cloned.1.call-start = ((), (), s32[]{:S(2)}) async-start(), calls=%async_computation | async-start | bytes 1622016 | tf_op jit(solution)/shard_map/all_gather | solution.py:164
  9.8 20.3 %collective-permute-start.1 = (f32[3,2,32,256]{3,2,1,0:T(8,128)}, f32[3,2,32,256]{3,2,1,0:T(8,128)S(1)}, u32[]{:S(2)}, u32[]{:S(2)}) collective-permute-start(f32[3,2,32,256]{3,2,1,0:T(8,128)} %get-tuple-element.218), channel_id=1, source_target_pairs={{4,0},{8,4},{12,8},{16,12},{20,16},{24,20},{28,24},{5,1},{9,5},{13... | collective-permute-start | bytes 589832 | tf_op jit(solution)/shard_map/ppermute | solution.py:28
  11.1 19.0 %collective-permute-start = (f32[3,2,32,256]{3,2,1,0:T(8,128)S(1)}, f32[3,2,32,256]{3,2,1,0:T(8,128)S(1)}, u32[]{:S(2)}, u32[]{:S(2)}) collective-permute-start(f32[3,2,32,256]{3,2,1,0:T(8,128)S(1)} %get-tuple-element.217), channel_id=1, source_target_pairs={{0,4},{4,8},{8,12},{12,16},{16,20},{20,24},{24,28},{1,5},{5,9},{9,... | collective-permute-start | bytes 589832 | tf_op jit(solution)/shard_map/ppermute | solution.py:26
  22.3 168.7 %all-gather.9.cloned.1.call-start = ((), (), s32[]{:S(2)}) async-start(), calls=%async_computation.1 | async-start | bytes 1622016 | tf_op jit(solution)/shard_map/all_gather | solution.py:164
  23.0 135.5 %copy-start.53 = (f32[256]{0:T(256)}, f32[256]{0:T(256)S(1)}, u32[]{:S(2)}) copy-start(f32[256]{0:T(256)S(1)} %get-tuple-element.265) | copy-start | bytes 3076
  23.0 141.2 %copy-start.51 = (f32[256]{0:T(256)}, f32[256]{0:T(256)S(1)}, u32[]{:S(2)}) copy-start(f32[256]{0:T(256)S(1)} %and_convert_fusion.2) | copy-start | bytes 3076
  23.6 140.7 %copy-start.49 = (f32[256]{0:T(256)}, f32[256]{0:T(256)S(1)}, u32[]{:S(2)}) copy-start(f32[256]{0:T(256)S(1)} %get-tuple-element.267) | copy-start | bytes 3076
  23.6 3.9 %copy-start.160 = (s32[16]{0:T(128)S(1)}, s32[16]{0:T(128)}, u32[]{:S(2)}) copy-start(s32[16]{0:T(128)} %get-tuple-element.230) | copy-start | bytes 196
  30.0 14.0 %copy-start.100 = (f32[8,32]{1,0:T(8,128)}, f32[8,32]{1,0:T(8,128)S(1)}, u32[]{:S(2)}) copy-start(f32[8,32]{1,0:T(8,128)S(1)} %get-tuple-element.247) | copy-start | bytes 3076
  30.0 17.4 %copy-start.82 = (f32[8,32]{1,0:T(8,128)}, f32[8,32]{1,0:T(8,128)S(1)}, u32[]{:S(2)}) copy-start(f32[8,32]{1,0:T(8,128)S(1)} %get-tuple-element.242) | copy-start | bytes 3076
  30.0 21.1 %copy-start.71 = (f32[8,32]{1,0:T(8,128)}, f32[8,32]{1,0:T(8,128)S(1)}, u32[]{:S(2)}) copy-start(f32[8,32]{1,0:T(8,128)S(1)} %get-tuple-element.240) | copy-start | bytes 3076
  30.0 23.1 %copy-start.64 = (f32[8,32]{1,0:T(8,128)}, f32[8,32]{1,0:T(8,128)S(1)}, u32[]{:S(2)}) copy-start(f32[8,32]{1,0:T(8,128)S(1)} %get-tuple-element.243) | copy-start | bytes 3076
  30.0 25.2 %copy-start.75 = (f32[8,32]{1,0:T(8,128)}, f32[8,32]{1,0:T(8,128)S(1)}, u32[]{:S(2)}) copy-start(f32[8,32]{1,0:T(8,128)S(1)} %get-tuple-element.238) | copy-start | bytes 3076
  30.0 26.2 %copy-start.58 = (f32[8,32]{1,0:T(8,128)}, f32[8,32]{1,0:T(8,128)S(1)}, u32[]{:S(2)}) copy-start(f32[8,32]{1,0:T(8,128)S(1)} %get-tuple-element.236) | copy-start | bytes 3076
  30.0 27.5 %copy-start.68 = (f32[8,32]{1,0:T(8,128)}, f32[8,32]{1,0:T(8,128)S(1)}, u32[]{:S(2)}) copy-start(f32[8,32]{1,0:T(8,128)S(1)} %get-tuple-element.239) | copy-start | bytes 3076
  30.0 28.6 %copy-start.61 = (f32[8,32]{1,0:T(8,128)}, f32[8,32]{1,0:T(8,128)S(1)}, u32[]{:S(2)}) copy-start(f32[8,32]{1,0:T(8,128)S(1)} %get-tuple-element.244) | copy-start | bytes 3076
  30.0 30.6 %copy-start.79 = (f32[8,32]{1,0:T(8,128)}, f32[8,32]{1,0:T(8,128)S(1)}, u32[]{:S(2)}) copy-start(f32[8,32]{1,0:T(8,128)S(1)} %get-tuple-element.235) | copy-start | bytes 3076
  30.0 11.1 %copy-start.20 = (f32[3,2,32,256]{3,2,1,0:T(8,128)}, f32[3,2,32,256]{3,2,1,0:T(8,128)S(1)}, u32[]{:S(2)}) copy-start(f32[3,2,32,256]{3,2,1,0:T(8,128)S(1)} %collective-permute-done.1) | copy-start | bytes 589828
  30.1 11.0 %collective-permute-start.3 = (f32[3,12,2,256]{3,2,1,0:T(2,128)S(1)}, f32[3,12,2,256]{3,2,1,0:T(2,128)S(1)}, u32[]{:S(2)}, u32[]{:S(2)}) collective-permute-start(f32[3,12,2,256]{3,2,1,0:T(2,128)S(1)} %get-tuple-element.190), channel_id=1, source_target_pairs={{1,0},{2,1},{3,2},{5,4},{6,5},{7,6},{9,8},{10,9},{11,10},{13,12},{... | collective-permute-start | bytes 221192 | tf_op jit(solution)/shard_map/ppermute | solution.py:28
  31.4 9.7 %collective-permute-start.2 = (f32[3,12,2,256]{3,2,1,0:T(2,128)S(1)}, f32[3,12,2,256]{3,2,1,0:T(2,128)S(1)}, u32[]{:S(2)}, u32[]{:S(2)}) collective-permute-start(f32[3,12,2,256]{3,2,1,0:T(2,128)S(1)} %get-tuple-element.191), channel_id=1, source_target_pairs={{0,1},{1,2},{2,3},{4,5},{5,6},{6,7},{8,9},{9,10},{10,11},{12,13},{... | collective-permute-start | bytes 221192 | tf_op jit(solution)/shard_map/ppermute | solution.py:26
  45.8 106.9 %copy-start.7 = (pred[1,8,32,256]{3,2,1,0:T(8,128)(4,1)}, pred[1,8,32,256]{3,2,1,0:T(8,128)(4,1)S(1)}, u32[]{:S(2)}) copy-start(pred[1,8,32,256]{3,2,1,0:T(8,128)(4,1)S(1)} %get-tuple-element.48) | copy-start | bytes 196612
  47.3 99.9 %copy-start.4 = (pred[1,8,32,256]{3,2,1,0:T(8,128)(4,1)}, pred[1,8,32,256]{3,2,1,0:T(8,128)(4,1)S(1)}, u32[]{:S(2)}) copy-start(pred[1,8,32,256]{3,2,1,0:T(8,128)(4,1)S(1)} %get-tuple-element.38) | copy-start | bytes 196612
  49.7 97.6 %copy-start.15 = (pred[1,8,32,256]{3,2,1,0:T(8,128)(4,1)}, pred[1,8,32,256]{3,2,1,0:T(8,128)(4,1)S(1)}, u32[]{:S(2)}) copy-start(pred[1,8,32,256]{3,2,1,0:T(8,128)(4,1)S(1)} %get-tuple-element.40) | copy-start | bytes 196612
  51.0 100.0 %copy-start.13 = (pred[1,8,32,256]{3,2,1,0:T(8,128)(4,1)}, pred[1,8,32,256]{3,2,1,0:T(8,128)(4,1)S(1)}, u32[]{:S(2)}) copy-start(pred[1,8,32,256]{3,2,1,0:T(8,128)(4,1)S(1)} %get-tuple-element.36) | copy-start | bytes 196612
  51.0 103.4 %copy-start.10 = (pred[1,8,32,256]{3,2,1,0:T(8,128)(4,1)}, pred[1,8,32,256]{3,2,1,0:T(8,128)(4,1)S(1)}, u32[]{:S(2)}) copy-start(pred[1,8,32,256]{3,2,1,0:T(8,128)(4,1)S(1)} %get-tuple-element.141) | copy-start | bytes 196612
  69.6 7.2 %collective-permute-start.5 = (f32[3,2,32,256]{3,2,1,0:T(8,128)}, f32[3,2,32,256]{3,2,1,0:T(8,128)S(1)}, u32[]{:S(2)}, u32[]{:S(2)}) collective-permute-start(f32[3,2,32,256]{3,2,1,0:T(8,128)} %get-tuple-element.211), channel_id=1, source_target_pairs={{4,0},{8,4},{12,8},{16,12},{20,16},{24,20},{28,24},{5,1},{9,5},{13... | collective-permute-start | bytes 589832 | tf_op jit(solution)/shard_map/ppermute | solution.py:28
  70.8 5.9 %collective-permute-start.4 = (f32[3,2,32,256]{3,2,1,0:T(8,128)S(1)}, f32[3,2,32,256]{3,2,1,0:T(8,128)S(1)}, u32[]{:S(2)}, u32[]{:S(2)}) collective-permute-start(f32[3,2,32,256]{3,2,1,0:T(8,128)S(1)} %get-tuple-element.210), channel_id=1, source_target_pairs={{0,4},{4,8},{8,12},{12,16},{16,20},{20,24},{24,28},{1,5},{5,9},{9,... | collective-permute-start | bytes 589832 | tf_op jit(solution)/shard_map/ppermute | solution.py:26
  76.8 17.2 %collective-permute-start.6 = (f32[3,12,2,256]{3,2,1,0:T(2,128)S(1)}, f32[3,12,2,256]{3,2,1,0:T(2,128)S(1)}, u32[]{:S(2)}, u32[]{:S(2)}) collective-permute-start(f32[3,12,2,256]{3,2,1,0:T(2,128)S(1)} %get-tuple-element.186), channel_id=1, source_target_pairs={{0,1},{1,2},{2,3},{4,5},{5,6},{6,7},{8,9},{9,10},{10,11},{12,13},{... | collective-permute-start | bytes 221192 | tf_op jit(solution)/shard_map/ppermute | solution.py:26
  81.1 12.9 %collective-permute-start.7 = (f32[3,12,2,256]{3,2,1,0:T(2,128)S(1)}, f32[3,12,2,256]{3,2,1,0:T(2,128)S(1)}, u32[]{:S(2)}, u32[]{:S(2)}) collective-permute-start(f32[3,12,2,256]{3,2,1,0:T(2,128)S(1)} %get-tuple-element.187), channel_id=1, source_target_pairs={{1,0},{2,1},{3,2},{5,4},{6,5},{7,6},{9,8},{10,9},{11,10},{13,12},{... | collective-permute-start | bytes 221192 | tf_op jit(solution)/shard_map/ppermute | solution.py:28
  128.5 86.3 %copy-start = (f32[3,8,32,256]{3,2,1,0:T(8,128)}, f32[3,8,32,256]{3,2,1,0:T(8,128)S(1)}, u32[]{:S(2)}) copy-start(f32[3,8,32,256]{3,2,1,0:T(8,128)S(1)} %get-tuple-element.25) | copy-start | bytes 2359300
  128.7 9.6 %copy-start.159 = (pred[16]{0:T(512)(128)(4,1)S(1)}, pred[16]{0:T(512)(128)(4,1)}, u32[]{:S(2)}) copy-start(pred[16]{0:T(512)(128)(4,1)} %get-tuple-element.23) | copy-start | bytes 52
  131.1 125.4 %all-gather.11.cloned.1.call-start = ((), (), s32[]{:S(2)}) async-start(), calls=%async_computation.2 | async-start | bytes 1622016 | tf_op jit(solution)/shard_map/all_gather | solution.py:164
  131.9 7.1 %collective-permute-start.9 = (f32[3,2,32,256]{3,2,1,0:T(8,128)S(1)}, f32[3,2,32,256]{3,2,1,0:T(8,128)S(1)}, u32[]{:S(2)}, u32[]{:S(2)}) collective-permute-start(f32[3,2,32,256]{3,2,1,0:T(8,128)S(1)} %get-tuple-element.204), channel_id=1, source_target_pairs={{4,0},{8,4},{12,8},{16,12},{20,16},{24,20},{28,24},{5,1},{9,5},{13... | collective-permute-start | bytes 589832 | tf_op jit(solution)/shard_map/ppermute | solution.py:28
  133.2 5.8 %collective-permute-start.8 = (f32[3,2,32,256]{3,2,1,0:T(8,128)S(1)}, f32[3,2,32,256]{3,2,1,0:T(8,128)S(1)}, u32[]{:S(2)}, u32[]{:S(2)}) collective-permute-start(f32[3,2,32,256]{3,2,1,0:T(8,128)S(1)} %get-tuple-element.203), channel_id=1, source_target_pairs={{0,4},{4,8},{8,12},{12,16},{16,20},{20,24},{24,28},{1,5},{5,9},{9,... | collective-permute-start | bytes 589832 | tf_op jit(solution)/shard_map/ppermute | solution.py:26
  139.0 13.7 %copy-start.22 = (f32[3,2,32,256]{3,2,1,0:T(8,128)}, f32[3,2,32,256]{3,2,1,0:T(8,128)S(1)}, u32[]{:S(2)}) copy-start(f32[3,2,32,256]{3,2,1,0:T(8,128)S(1)} %collective-permute-done.9) | copy-start | bytes 589828
  139.0 11.7 %copy-start.18 = (f32[3,2,32,256]{3,2,1,0:T(8,128)}, f32[3,2,32,256]{3,2,1,0:T(8,128)S(1)}, u32[]{:S(2)}) copy-start(f32[3,2,32,256]{3,2,1,0:T(8,128)S(1)} %collective-permute-done.8) | copy-start | bytes 589828
  139.1 16.9 %collective-permute-start.10 = (f32[3,12,2,256]{3,2,1,0:T(2,128)S(1)}, f32[3,12,2,256]{3,2,1,0:T(2,128)S(1)}, u32[]{:S(2)}, u32[]{:S(2)}) collective-permute-start(f32[3,12,2,256]{3,2,1,0:T(2,128)S(1)} %get-tuple-element.182), channel_id=1, source_target_pairs={{0,1},{1,2},{2,3},{4,5},{5,6},{6,7},{8,9},{9,10},{10,11},{12,13},{... | collective-permute-start | bytes 221192 | tf_op jit(solution)/shard_map/ppermute | solution.py:26
  143.4 12.6 %collective-permute-start.11 = (f32[3,12,2,256]{3,2,1,0:T(2,128)S(1)}, f32[3,12,2,256]{3,2,1,0:T(2,128)S(1)}, u32[]{:S(2)}, u32[]{:S(2)}) collective-permute-start(f32[3,12,2,256]{3,2,1,0:T(2,128)S(1)} %get-tuple-element.183), channel_id=1, source_target_pairs={{1,0},{2,1},{3,2},{5,4},{6,5},{7,6},{9,8},{10,9},{11,10},{13,12},{... | collective-permute-start | bytes 221192 | tf_op jit(solution)/shard_map/ppermute | solution.py:28
  165.9 27.2 %copy-start.48 = (f32[32,3,128]{2,0,1:T(8,128)S(1)}, f32[32,3,128]{2,0,1:T(8,128)}, u32[]{:S(2)}) copy-start(f32[32,3,128]{2,0,1:T(8,128)} %copy-done.46) | copy-start | bytes 147460
  198.8 3.8 %copy-start.52 = (f32[256]{0:T(256)S(1)}, f32[256]{0:T(256)}, u32[]{:S(2)}) copy-start(f32[256]{0:T(256)} %copy-done.51) | copy-start | bytes 3076
  198.8 3.8 %copy-start.54 = (f32[256]{0:T(256)S(1)}, f32[256]{0:T(256)}, u32[]{:S(2)}) copy-start(f32[256]{0:T(256)} %copy-done.53) | copy-start | bytes 3076
  198.9 3.8 %copy-start.63 = (f32[8,32]{1,0:T(8,128)S(1)}, f32[8,32]{1,0:T(8,128)}, u32[]{:S(2)}) copy-start(f32[8,32]{1,0:T(8,128)} %copy-done.61) | copy-start | bytes 3076
  224.8 33.2 %copy-start.55 = (f32[32,3,128]{2,0,1:T(8,128)S(1)}, f32[32,3,128]{2,0,1:T(8,128)}, u32[]{:S(2)}) copy-start(f32[32,3,128]{2,0,1:T(8,128)} %reduce_sum.115) | copy-start | bytes 147460
  224.9 33.2 %copy-start.56 = (f32[32,3,128]{2,0,1:T(8,128)S(1)}, f32[32,3,128]{2,0,1:T(8,128)}, u32[]{:S(2)}) copy-start(f32[32,3,128]{2,0,1:T(8,128)} %get-tuple-element.30) | copy-start | bytes 147460
  (139 other events, 254.1 us)
Sparse Core Ops, SparseCore 0:
  22.4 57.8 all-gather.6
  131.2 59.7 all-gather.8
  202.8 53.7 all-gather.10
